TPU v7x, 512 devices: a whole 4x8x8 slice. The times are simulated.
512 devices in a mesh: dp: 2 (over core), seq: 64 (over y, z), tensor: 4 (over x).
Axes of the slice: x: 4, y: 8, z: 8, core: 2. Of those that a mesh axis runs over, the one named last changes fastest.
Arguments:
- query: bfloat16 [2, 16384, 2048], P('dp', 'seq', 'tensor'), may hold values from -1.75 to 1.75
- key_rows: bfloat16 [2, 16384, 2048], P('dp', 'seq', 'tensor'), may hold values from -1.75 to 1.75
- value: bfloat16 [2, 16384, 2048], P('dp', 'seq', 'tensor'), may hold values from -40 to 40
- gain: float32 [2048], P('tensor'), may hold values from 0.25 to 1.75
- grad_out: bfloat16 [2, 16384, 2048], P('dp', 'seq', 'tensor'), may hold values from -16 to 16
- start_offset: int32 [2, 256], P('dp', 'seq'), may hold values from 0 to 64, as said below
Outputs:
- attn_out: bfloat16 [2, 16384, 2048], P('dp', 'seq', 'tensor')
- grad_query: bfloat16 [2, 16384, 2048], P('dp', 'seq', 'tensor')
- grad_key: bfloat16 [2, 16384, 2048], P('dp', 'seq', 'tensor')
- grad_value: bfloat16 [2, 16384, 2048], P('dp', 'seq', 'tensor')
- grad_gain: float32 [2048], P('tensor')
Inputs may be any that keep to these rules, and one draw needn't show every extreme that they name: `start_offset`: the position within its block of 64 positions at which a document starts; 64 when none starts in the block; every sequence begins a document at its first position.
All inputs are finite; a program needn't handle non-finite values.
Results may differ from a plain program's by a relative error of at most 0.0058.
Values sent between devices are 32-bit elements; how exact they have to be, the bound alone decides.
No kernel may reach another device: no remote copies, remote signals or barrier semaphores. Data moves between devices by JAX's collectives and lax.ppermute only.
A program may use at most 64 MiB of HBM per device.

v0:
```python
import jax
import jax.numpy as jnp
from jax import lax
from jax.sharding import PartitionSpec as P

DH = 128
BLK = 64
CH = 2048
eps_value = 1e-05


def carried_in(part, axis, combine, identity, reverse):
    count = lax.axis_size(axis)
    place = lax.axis_index(axis)
    ahead = count - 1 - place if reverse else place
    gathered = jax.tree.map(lambda a: lax.all_gather(a, axis), part)
    state = jax.tree.map(lambda a, e: jnp.zeros_like(a) + jnp.asarray(e, a.dtype), part, identity)

    def one(turn, state):
        source = count - 1 - turn if reverse else turn
        return combine(
            state, jax.tree.map(lambda a: lax.dynamic_index_in_dim(a, source, 0, False), gathered)
        )

    return lax.fori_loop(0, ahead, one, state)


def segment_rows(offsets, length_dev):
    positions = jnp.arange(length_dev, dtype=jnp.int32)
    block_starts = jnp.arange(offsets.shape[0], dtype=jnp.int32) * BLK + offsets
    present = offsets < BLK
    covered = (block_starts[None, :] <= positions[:, None]) & present[None, :]
    labels = jnp.sum(covered.astype(jnp.int32), axis=1)
    allowed = (labels[:, None] == labels[None, :]) & (positions[None, :] <= positions[:, None])
    starts = jnp.sum(present.astype(jnp.int32))
    return (labels, starts, allowed)


def joined(earlier, later):
    return (
        jnp.where(later[1] > 0, later[0], earlier[0] + later[0]),
        jnp.maximum(earlier[1], later[1]),
    )


def shards(query, key_rows, value, gain, grad_out, start_offset):
    length_dev = query.shape[1]
    width_local = query.shape[2]
    heads_local = width_local // DH
    query_heads = query[0].reshape(length_dev, heads_local, DH)
    key_heads = key_rows[0].reshape(length_dev, heads_local, DH)
    value_heads = value[0].reshape(length_dev, heads_local, DH)
    labels, starts, allowed = segment_rows(start_offset[0], length_dev)
    head_mask = (labels == 0)[:, None, None]
    tail_mask = (labels == starts)[:, None, None]
    reset = (starts > 0).astype(jnp.int32)
    scores = jnp.einsum("thd,shd->hts", query_heads, key_heads, preferred_element_type=jnp.float32)
    weights = jnp.where(allowed[None], scores, 0.0).astype(jnp.bfloat16)
    local_out = jnp.einsum("hts,shd->thd", weights, value_heads, preferred_element_type=jnp.float32)
    tail_keys = jnp.where(tail_mask, key_heads, jnp.zeros_like(key_heads))
    tail_values = jnp.where(tail_mask, value_heads, jnp.zeros_like(value_heads))
    tail_state = jnp.einsum(
        "shi,shj->hij", tail_keys, value_heads, preferred_element_type=jnp.float32
    )
    zero_state = jnp.zeros_like(tail_state)
    incoming = carried_in((tail_state, reset), "seq", joined, (zero_state, jnp.int32(0)), False)[0]
    carried = incoming.astype(jnp.bfloat16)
    head_query = jnp.where(head_mask, query_heads, jnp.zeros_like(query_heads))
    carried_out = jnp.einsum(
        "thi,hij->thj", head_query, carried, preferred_element_type=jnp.float32
    )
    attended = (local_out + carried_out).reshape(length_dev, width_local)
    upstream = grad_out[0].astype(jnp.float32)
    scaled = gain[None, :] * upstream
    square_local = jnp.sum(attended * attended, axis=1)
    square_total = lax.psum(square_local, "tensor")
    inverse = lax.rsqrt(square_total / CH + eps_value)
    normed = attended * inverse[:, None]
    product_total = lax.psum(jnp.sum(scaled * normed, axis=1), "tensor")
    output = (gain[None, :] * normed).astype(jnp.bfloat16)
    grad_pre = (inverse[:, None] * (scaled - normed * (product_total / CH)[:, None])).astype(
        jnp.bfloat16
    )
    gain_local = jnp.sum(upstream * normed, axis=0)
    grad_gain = lax.psum(gain_local, ("dp", "seq"))
    grad_heads = grad_pre.reshape(length_dev, heads_local, DH)
    grad_state = jnp.einsum(
        "thi,thj->hij", head_query, grad_heads, preferred_element_type=jnp.float32
    )
    later = carried_in((grad_state, reset), "seq", joined, (zero_state, jnp.int32(0)), True)[0]
    later_half = later.astype(jnp.bfloat16)
    grad_scores = jnp.einsum(
        "thd,shd->hts", grad_heads, value_heads, preferred_element_type=jnp.float32
    )
    grad_weights = jnp.where(allowed[None], grad_scores, 0.0).astype(jnp.bfloat16)
    head_grad = jnp.where(head_mask, grad_heads, jnp.zeros_like(grad_heads))
    grad_query = jnp.einsum(
        "hts,shd->thd", grad_weights, key_heads, preferred_element_type=jnp.float32
    ) + jnp.einsum("thj,hij->thi", head_grad, carried, preferred_element_type=jnp.float32)
    grad_key = jnp.einsum(
        "hts,thd->shd", grad_weights, query_heads, preferred_element_type=jnp.float32
    ) + jnp.einsum("shj,hij->shi", tail_values, later_half, preferred_element_type=jnp.float32)
    grad_value = jnp.einsum(
        "hts,thd->shd", weights, grad_heads, preferred_element_type=jnp.float32
    ) + jnp.einsum("shi,hij->shj", tail_keys, later_half, preferred_element_type=jnp.float32)
    shape_dev = (1, length_dev, width_local)
    return (
        output.reshape(shape_dev),
        grad_query.reshape(shape_dev).astype(jnp.bfloat16),
        grad_key.reshape(shape_dev).astype(jnp.bfloat16),
        grad_value.reshape(shape_dev).astype(jnp.bfloat16),
        grad_gain,
    )


def solution(mesh):
    return jax.shard_map(
        shards,
        mesh=mesh,
        in_specs=(
            P("dp", "seq", "tensor"),
            P("dp", "seq", "tensor"),
            P("dp", "seq", "tensor"),
            P("tensor"),
            P("dp", "seq", "tensor"),
            P("dp", "seq"),
        ),
        out_specs=(
            P("dp", "seq", "tensor"),
            P("dp", "seq", "tensor"),
            P("dp", "seq", "tensor"),
            P("dp", "seq", "tensor"),
            P("tensor"),
        ),
        check_vma=False,
    )
```

profile of v0, /device:TPU:1, one launch (start us, length us, event | category | flops | bytes accessed | tf_op | source)
XLA Modules:
  0.0 739.9 jit_solution(13396427716960763037)
XLA Ops:
  7.9 1.3 fusion.29
  9.2 1.1 copy.54
  10.3 1.1 copy.57
  13.8 1.1 copy.53
  14.9 1.1 copy.62
  15.9 1.3 dynamic-slice
  18.0 26.8 %all-reduce = s32[64]{0:T(128)S(1)} all-reduce(s32[64]{0:T(128)S(1)} %dynamic-update-slice), channel_id=1, replica_groups=mesh['dp'=2,'seq'=64,'tensor'=4] {'seq'}, use_global_device_ids=true, to_apply=%add | all-reduce | flops 64 | bytes 512
  45.6 112.6 %all-gather.5.cloned.1.call-done = f32[256,128,128]{2,1,0:T(8,128)} async-done(((f32[4,128,128]{2,1,0:T(8,128)}), f32[256,128,128]{2,1,0:T(8,128)}) %all-gather.5.cloned.1.call-update) | async-done | bytes 16777232 | tf_op jit(solution)/shard_map/all_gather | solution.py:16
  158.5 8.4 %psum.21 = f32[256]{0:T(256)S(1)} all-reduce(f32[256]{0:T(256)S(1)} %get-tuple-element.176), channel_id=1, replica_groups=mesh['dp'=2,'seq'=64,'tensor'=4] {'tensor'}, use_global_device_ids=true, to_apply=%region_5.6 | all-reduce | flops 256 | bytes 2048 | tf_op jit(solution)/shard_map/psum | solution.py:76
  167.1 1.2 fusion.10
  168.3 6.0 psum.22
  178.1 405.6 %psum.23 = f32[512]{0:T(512)} all-reduce(f32[512]{0:T(512)S(1)} %get-tuple-element.150), channel_id=1, replica_groups=mesh['dp'=2,'seq'=64,'tensor'=4] {'dp','seq'}, use_global_device_ids=true, to_apply=%region_11.12 | all-reduce | flops 512 | bytes 4096 | tf_op jit(solution)/shard_map/psum | solution.py:85
  585.0 145.9 %while.27 = (s32[]{:T(128)}, f32[4,128,128]{2,1,0:T(8,128)S(1)}, s32[]{:T(128)}, s32[64]{0:T(128)S(1)}, f32[64,4,128,128]{3,2,1,0:T(8,128)}, /*index=5*/s32[]{:T(128)}, s32[]{:T(128)}, s32[]{:T(128)}, s32[]{:T(128)}, s32[1]{0:T(128)}) while((s32[]{:T(128)}, f32[4,128,128]{2,1,0:T(8,128)S(1)}, s32[]{:T(128)}, s32[64]{0:T(128)S(1)}, ...), condition=%wide.region_9.10_spmd, body=%wide.region_8.9_spmd.sunk | while | flops 131079 | bytes 786613 | solution.py:25
  586.3 1.1 add_select_fusion.5
  588.6 1.1 add_select_fusion.5
  590.9 1.1 add_select_fusion.5
  595.5 1.1 add_select_fusion.5
  600.2 1.1 add_select_fusion.5
  604.8 1.1 add_select_fusion.5
  609.4 1.1 add_select_fusion.5
  614.1 1.1 add_select_fusion.5
  618.7 1.1 add_select_fusion.5
  623.3 1.1 add_select_fusion.5
  625.7 1.1 add_select_fusion.5
  (152 shorter events, 103.4 us)
Async XLA Ops:
  7.2 576.5 %copy-start = (f32[512]{0:T(512)S(1)}, f32[512]{0:T(512)}, u32[]{:S(2)}) copy-start(f32[512]{0:T(512)} %param.13) | copy-start | bytes 6148
  7.2 151.0 %all-gather.5.cloned.1.call-start = ((), (), s32[]{:S(2)}) async-start(), calls=%async_computation | async-start | bytes 17039360 | tf_op jit(solution)/shard_map/all_gather | solution.py:16
  13.1 571.9 %all-gather.7.cloned.1.call-start = ((), (), s32[]{:S(2)}) async-start(), calls=%async_computation.1 | async-start | bytes 17039360 | tf_op jit(solution)/shard_map/all_gather | solution.py:16
Sparse Core Ops, SparseCore 0:
  13.2 144.9 all-gather.4
  176.2 284.0 all-gather.6
where the time goes:
time: 743 us; the launch traced here: 740 us
  blocking collectives  447 us (60%)
  waiting for transfers between devices  113 us (15%)
  other arithmetic  71.9 us (10%)
  local copies, waits for them, and re-layouts  46.4 us (6%)
  loops' own time  42.6 us (6%)
  between operations  14.9 us (2%)
    psum x1, blocking collectives, shards(): grad_gain = lax.psum(gain_local, ('dp', 'seq'))  406 us
    all_gather x2, waiting for transfers between devices, carried_in(): gathered = jax.tree.map(lambda a: lax.all_gather(a, axis), part)  113 us
    select_n x63, other arithmetic, joined(): jnp.where(later[1] > 0, later[0], earlier[0] + later[0])  66.2 us
    another operation x2, loops' own time, carried_in(): return lax.fori_loop(0, ahead, one, state)  42.6 us
    dynamic_slice x63, local copies, waits for them, and re-layouts, one(): lax.dynamic_index_in_dim(a, source, 0, False)  37.1 us
    unnamed x1, blocking collectives  26.8 us
  transfers between devices with their start and end apart: 2, of which 1 were waited for; matrix products, arithmetic and copies ran while one was open for 1% of the time, Pallas kernels for 0%

commit v1 on v0

--- a/solution.py
+++ b/solution.py
@@ -82,7 +82,7 @@
         jnp.bfloat16
     )
     gain_local = jnp.sum(upstream * normed, axis=0)
-    grad_gain = lax.psum(gain_local, ("dp", "seq"))
+    grad_gain = lax.psum(lax.psum(gain_local, "dp"), "seq")
     grad_heads = grad_pre.reshape(length_dev, heads_local, DH)
     grad_state = jnp.einsum(
         "thi,thj->hij", head_query, grad_heads, preferred_element_type=jnp.float32

time: 743 us -> 636 us (0.86)
  the two profiles are of different devices: /device:TPU:1 before, /device:TPU:2 now
where the time goes in v1:
time: 636 us; the launch traced here: 633 us
  blocking collectives  344 us (54%)
  waiting for transfers between devices  108 us (17%)
  other arithmetic  71.9 us (11%)
  local copies, waits for them, and re-layouts  46.4 us (7%)
  loops' own time  42.6 us (7%)
  between operations  14.9 us (2%)
    psum x2, blocking collectives, shards(): grad_gain = lax.psum(lax.psum(gain_local, 'dp'), 'seq')  295 us
    all_gather x2, waiting for transfers between devices, carried_in(): gathered = jax.tree.map(lambda a: lax.all_gather(a, axis), part)  108 us
    select_n x63, other arithmetic, joined(): jnp.where(later[1] > 0, later[0], earlier[0] + later[0])  66.2 us
    another operation x2, loops' own time, carried_in(): return lax.fori_loop(0, ahead, one, state)  42.6 us
    dynamic_slice x63, local copies, waits for them, and re-layouts, one(): lax.dynamic_index_in_dim(a, source, 0, False)  37.1 us
    unnamed x1, blocking collectives  31 us
  transfers between devices with their start and end apart: 2, of which 1 were waited for; matrix products, arithmetic and copies ran while one was open for 1% of the time, Pallas kernels for 0%

profile of v1, /device:TPU:2, one launch (start us, length us, event | category | flops | bytes accessed | tf_op | source)
XLA Modules:
  0.0 632.5 jit_solution(12725390414444873696)
XLA Ops:
  7.9 1.3 fusion.29
  9.2 1.1 copy.54
  10.3 1.1 copy.57
  13.8 1.1 copy.53
  14.9 1.1 copy.62
  15.9 1.3 dynamic-slice
  18.0 31.0 %all-reduce = s32[64]{0:T(128)S(1)} all-reduce(s32[64]{0:T(128)S(1)} %dynamic-update-slice), channel_id=1, replica_groups=mesh['dp'=2,'seq'=64,'tensor'=4] {'seq'}, use_global_device_ids=true, to_apply=%add | all-reduce | flops 64 | bytes 512
  49.8 107.7 %all-gather.5.cloned.1.call-done = f32[256,128,128]{2,1,0:T(8,128)} async-done(((f32[4,128,128]{2,1,0:T(8,128)}), f32[256,128,128]{2,1,0:T(8,128)}) %all-gather.5.cloned.1.call-update) | async-done | bytes 16777232 | tf_op jit(solution)/shard_map/all_gather | solution.py:16
  157.8 8.6 %psum.28 = f32[256]{0:T(256)S(1)} all-reduce(f32[256]{0:T(256)S(1)} %get-tuple-element.176), channel_id=1, replica_groups=mesh['dp'=2,'seq'=64,'tensor'=4] {'tensor'}, use_global_device_ids=true, to_apply=%region_5.6 | all-reduce | flops 256 | bytes 2048 | tf_op jit(solution)/shard_map/psum | solution.py:76
  166.6 1.2 fusion.10
  167.8 10.1 %psum.29 = f32[256]{0:T(256)S(1)} all-reduce(f32[256]{0:T(256)S(1)} %get-tuple-element.151), channel_id=1, replica_groups=mesh['dp'=2,'seq'=64,'tensor'=4] {'tensor'}, use_global_device_ids=true, to_apply=%region_7.8 | all-reduce | flops 256 | bytes 2048 | tf_op jit(solution)/shard_map/psum | solution.py:79
  181.7 2.4 psum.30
  184.1 292.2 %psum.31 = f32[512]{0:T(512)} all-reduce(f32[512]{0:T(512)S(1)} %psum.30), channel_id=1, replica_groups=mesh['dp'=2,'seq'=64,'tensor'=4] {'seq'}, use_global_device_ids=true, to_apply=%region_12.13 | all-reduce | flops 512 | bytes 4096 | tf_op jit(solution)/shard_map/psum | solution.py:85
  477.6 145.9 %while.27 = (s32[]{:T(128)}, f32[4,128,128]{2,1,0:T(8,128)S(1)}, s32[]{:T(128)}, s32[64]{0:T(128)S(1)}, f32[64,4,128,128]{3,2,1,0:T(8,128)}, /*index=5*/s32[]{:T(128)}, s32[]{:T(128)}, s32[]{:T(128)}, s32[]{:T(128)}, s32[1]{0:T(128)}) while((s32[]{:T(128)}, f32[4,128,128]{2,1,0:T(8,128)S(1)}, s32[]{:T(128)}, s32[64]{0:T(128)S(1)}, ...), condition=%wide.region_9.10_spmd, body=%wide.region_8.9_spmd.sunk | while | flops 131079 | bytes 786613 | solution.py:25
  481.2 1.1 add_select_fusion.5
  483.5 1.1 add_select_fusion.5
  485.8 1.1 add_select_fusion.5
  488.1 1.1 add_select_fusion.5
  490.5 1.1 add_select_fusion.5
  492.8 1.1 add_select_fusion.5
  497.4 1.1 add_select_fusion.5
  502.0 1.1 add_select_fusion.5
  506.7 1.1 add_select_fusion.5
  511.3 1.1 add_select_fusion.5
  (153 shorter events, 104.5 us)
Async XLA Ops:
  7.2 469.1 %copy-start = (f32[512]{0:T(512)S(1)}, f32[512]{0:T(512)}, u32[]{:S(2)}) copy-start(f32[512]{0:T(512)} %param.13) | copy-start | bytes 6148
  7.2 150.3 %all-gather.5.cloned.1.call-start = ((), (), s32[]{:S(2)}) async-start(), calls=%async_computation | async-start | bytes 17039360 | tf_op jit(solution)/shard_map/all_gather | solution.py:16
  13.1 464.5 %all-gather.7.cloned.1.call-start = ((), (), s32[]{:S(2)}) async-start(), calls=%async_computation.1 | async-start | bytes 17039360 | tf_op jit(solution)/shard_map/all_gather | solution.py:16
Sparse Core Ops, SparseCore 0:
  13.2 144.2 all-gather.4
  179.9 279.6 all-gather.6
